TPU v7x, 32 devices: a whole 2x2x4 slice. The times are simulated.
32 devices in a mesh: groups: 2 (over y), seq: 8 (over z, x), head: 2 (over core).
Axes of the slice: x: 2, y: 2, z: 4, core: 2. Of those that a mesh axis runs over, the one named last changes fastest.
Arguments:
- queries: bfloat16 [256, 3072], P(('groups', 'seq'), 'head'), parts along dimension 0, may hold values from -300 to 300, as said below
- latent: bfloat16 [512, 256], P(None, ('groups', 'seq')), parts along dimension 1, may hold values from -6 to 6
- key_basis: bfloat16 [512, 3072], P(None, 'head'), may hold values from -0.25 to 0.25
- value_basis: bfloat16 [512, 3072], P(None, 'head'), may hold values from -0.25 to 0.25
- out_weight: bfloat16 [3072, 3072], P('seq', 'head'), may hold values from -0.625 to 0.625
Outputs:
- attended: bfloat16 [256, 3072], P(('groups', 'seq'), 'head'), parts along dimension 0
There are 2 independent parts, one for each index of `groups`. A program takes and returns all parts, laid end to end along the dimension named above; an argument that names none is the same for every part. Nothing has to cross between parts.
Inputs may be any that keep to these rules, and one draw needn't show every extreme that they name: `queries`: real-valued entries.
All inputs are finite; a program needn't handle non-finite values.
Results may differ from a plain program's by a relative error of at most 0.0099.
Values may be sent and summed in bfloat16 or wider, within the bound.
A program may use at most 64 MiB of HBM per device.

v0:
```python
import math

import jax
import jax.numpy as jnp
from jax import lax
from jax.sharding import PartitionSpec as P

HEAD_DIM = 128


def attend(queries, latent, key_basis, value_basis):
    tok_rows = queries.shape[0]
    head_count = key_basis.shape[1] // HEAD_DIM
    rank_count = key_basis.shape[0]
    score_scale = 1.0 / math.sqrt(HEAD_DIM)
    query_heads = queries.reshape(tok_rows, head_count, HEAD_DIM).transpose(1, 0, 2)
    key_maps = key_basis.reshape(rank_count, head_count, HEAD_DIM).transpose(1, 0, 2)
    value_maps = value_basis.reshape(rank_count, head_count, HEAD_DIM).transpose(1, 0, 2)

    def one_head(operands):
        query_one, key_map, value_map = operands
        key_rows = lax.dot_general(
            latent, key_map, (((0,), (0,)), ((), ())), preferred_element_type=jnp.float32
        ).astype(jnp.bfloat16)
        value_rows = lax.dot_general(
            latent, value_map, (((0,), (0,)), ((), ())), preferred_element_type=jnp.float32
        ).astype(jnp.bfloat16)
        scores = (
            lax.dot_general(
                query_one, key_rows, (((1,), (1,)), ((), ())), preferred_element_type=jnp.float32
            )
            * score_scale
        )
        row_max = jnp.max(scores, axis=1, keepdims=True)
        weights = jnp.exp(scores - row_max)
        row_total = jnp.sum(weights, axis=1, keepdims=True)
        head_mixed = (
            jnp.dot(weights.astype(jnp.bfloat16), value_rows, preferred_element_type=jnp.float32)
            / row_total
        )
        return head_mixed.astype(jnp.bfloat16)

    mixed = lax.map(one_head, (query_heads, key_maps, value_maps))
    return mixed.transpose(1, 0, 2).reshape(tok_rows, head_count * HEAD_DIM)


def shards(queries, latent, key_basis, value_basis, out_weight):
    gathered = lax.all_gather(latent, "seq", axis=1, tiled=True)
    attended_heads = attend(queries, gathered, key_basis, value_basis)
    partial_value = lax.dot_general(
        attended_heads,
        lax.all_gather(out_weight, "seq", axis=0, tiled=True),
        (((1,), (1,)), ((), ())),
        preferred_element_type=jnp.float32,
    )
    attended = lax.psum_scatter(partial_value, "head", scatter_dimension=1, tiled=True).astype(
        jnp.bfloat16
    )
    return attended


def solution(mesh):
    placed = (
        P(("groups", "seq"), "head"),
        P(None, ("groups", "seq")),
        P(None, "head"),
        P(None, "head"),
        P("seq", "head"),
    )
    return jax.shard_map(
        shards, mesh=mesh, in_specs=placed, out_specs=P(("groups", "seq"), "head"), check_vma=False
    )
```

profile of v0, /device:TPU:1, one launch (start us, length us, event | category | flops | bytes accessed | tf_op | source)
XLA Modules:
  0.0 171.3 jit_solution(4047523913537241126)
XLA Ops:
  6.5 0.7 all-gather.2.cloned.1.call-update
  7.3 0.0 reduce-scatter.2.cloned.1.call-start
  7.3 1.7 %copy.14 = bf16[512,1536]{0,1:T(8,128)(2,1)S(1)} copy(bf16[512,1536]{1,0:T(8,128)(2,1)} %param.9) | data formatting | bytes 3145728 | tf_op args[2]
  9.1 1.7 %copy.15 = bf16[512,1536]{0,1:T(8,128)(2,1)S(1)} copy(bf16[512,1536]{1,0:T(8,128)(2,1)} %param.10) | data formatting | bytes 3145728 | tf_op args[3]
  10.8 26.8 %all_gather.6 = bf16[512,128]{0,1:T(8,128)(2,1)S(1)} all-gather(bf16[512,16]{0,1:T(8,128)(2,1)S(1)} %copy-done.1), channel_id=1, replica_groups=mesh['groups'=2,'seq'=8,'head'=2] {'seq'}, dimensions={1}, use_global_device_ids=true | all-gather | bytes 147456 | tf_op jit(solution)/shard_map/all_gather | solution.py:48
  37.6 0.1 copy.18
  37.8 0.1 reshape.14
  37.8 10.8 %while.10 = (s32[]{:T(128)}, bf16[12,16,128]{2,1,0:T(8,128)(2,1)S(1)}, bf16[12,16,128]{2,1,0:T(8,128)(2,1)S(1)}, bf16[12,512,128]{1,2,0:T(8,128)(2,1)S(1)}, bf16...) while((s32[]{:T(128)}, bf16[12,16,128]{2,1,0:T(8,128)(2,1)S(1)}, ...), condition=%wide.region_3.4_spmd, body=%wide.region_0.3_spmd.sunk | while | flops 34652128 | bytes 560397 | solution.py:43
  37.9 0.4 fusion.48
  38.2 0.2 fusion.49
  38.4 0.3 fusion.50
  38.7 0.4 fusion.48
  39.1 0.2 fusion.49
  39.3 0.3 fusion.50
  39.6 0.4 fusion.48
  40.1 0.2 fusion.49
  40.2 0.3 fusion.50
  40.5 0.4 fusion.48
  41.0 0.2 fusion.49
  41.1 0.3 fusion.50
  41.4 0.4 fusion.48
  41.9 0.2 fusion.49
  42.0 0.3 fusion.50
  42.3 0.4 fusion.48
  42.8 0.2 fusion.49
  42.9 0.3 fusion.50
  43.3 0.4 fusion.48
  43.7 0.2 fusion.49
  43.8 0.3 fusion.50
  44.2 0.4 fusion.48
  44.6 0.2 fusion.49
  44.7 0.3 fusion.50
  45.1 0.4 fusion.48
  45.5 0.2 fusion.49
  45.6 0.3 fusion.50
  46.0 0.4 fusion.48
  46.4 0.2 fusion.49
  46.6 0.3 fusion.50
  46.9 0.4 fusion.48
  47.3 0.2 fusion.49
  47.5 0.3 fusion.50
  47.8 0.4 fusion.48
  48.2 0.2 fusion.49
  48.4 0.3 fusion.50
  48.7 100.3 %all-gather.2.cloned.1.call-done = bf16[3072,1536]{1,0:T(8,128)(2,1)} async-done(((bf16[384,1536]{1,0:T(8,128)(2,1)}), bf16[3072,1536]{1,0:T(8,128)(2,1)}) %all-gather.2.cloned.1.call-update) | async-done | bytes 9437200 | tf_op jit(solution)/shard_map/all_gather | solution.py:52
  148.9 6.9 %fusion.25 = f32[16,3072]{1,0:T(8,128)} fusion(bf16[3072,1536]{1,0:T(8,128)(2,1)} %all-gather.2.cloned.1.call-done, bf16[12,16,128]{2,1,0:T(8,128)(2,1)S(1)} %get-tuple-element.37), kind=kOutput, calls=%fused_computation.21 | convolution fusion | flops 150994944 | bytes 9682944 | tf_op jit(solution)/shard_map/dot_general | solution.py:50
  155.9 7.1 %reduce-scatter.2.cloned.1.call-done = f32[16,1536]{1,0:T(8,128)} async-done(((f32[16,3072]{1,0:T(8,128)}), f32[16,1536]{1,0:T(8,128)}) %reduce-scatter.2.cloned.1.call-update) | async-done | bytes 98320 | tf_op jit(solution)/shard_map/reduce_scatter | solution.py:56
  162.9 1.5 convert_element_type.17
  (8 shorter events, 0.0 us)
Async XLA Ops:
  6.5 142.4 %all-gather.2.cloned.1.call-start = ((), (), s32[]{:S(2)}) async-start(), calls=%async_computation.1 | async-start | bytes 10616832 | tf_op jit(solution)/shard_map/all_gather | solution.py:52
  7.3 155.7 %reduce-scatter.2.cloned.1.call-start = ((), (), s32[]{:S(2)}) async-start(), calls=%async_computation.2 | async-start | bytes 294912 | tf_op jit(solution)/shard_map/reduce_scatter | solution.py:56
  9.0 1.8 %copy-start.1 = (bf16[512,16]{0,1:T(8,128)(2,1)S(1)}, bf16[512,16]{0,1:T(8,128)(2,1)}, u32[]{:S(2)}) copy-start(bf16[512,16]{0,1:T(8,128)(2,1)} %param.8) | copy-start | bytes 49156
  9.0 28.7 %copy-start = (bf16[16,1536]{1,0:T(8,128)(2,1)S(1)}, bf16[16,1536]{1,0:T(8,128)(2,1)}, u32[]{:S(2)}) copy-start(bf16[16,1536]{1,0:T(8,128)(2,1)} %param.7) | copy-start | bytes 147460
Sparse Core Ops, SparseCore 0:
  9.5 139.3 all-gather.1
  156.0 6.8 reduce-scatter.1
where the time goes:
time: 172 us; the launch traced here: 171 us
  waiting for transfers between devices  108 us (63%)
  blocking collectives  26.8 us (16%)
  matrix products  15.4 us (9%)
  between operations  13.5 us (8%)
  other arithmetic  3.78 us (2%)
  local copies, waits for them, and re-layouts  3.65 us (2%)
    all_gather x1, waiting for transfers between devices, shards(): lax.all_gather(out_weight, 'seq', axis=0, tiled=True)  100 us
    all_gather x1, blocking collectives, shards(): gathered = lax.all_gather(latent, 'seq', axis=1, tiled=True)  26.8 us
    reduce_scatter x1, waiting for transfers between devices, shards(): lax.psum_scatter(partial_value, 'head', scatter_dimension=1, tiled=True)  7.06 us
    dot_general x1, matrix products, shards(): lax.dot_general(attended_heads, lax.all_gather(out_weight, 'seq', axis=0,...  6.91 us
    dot_general x12, matrix products, one_head(): lax.dot_general(query_one, key_rows, (((1,), (1,)), ((), ())), preferred_...  4.84 us
    dot_general x12, matrix products, one_head(): jnp.dot(weights.astype(jnp.bfloat16), value_rows, preferred_element_type=...  3.64 us
    unnamed x6, local copies, waits for them, and re-layouts  3.46 us
  transfers between devices with their start and end apart: 2, of which 2 were waited for; matrix products, arithmetic and copies ran while one was open for 8% of the time, Pallas kernels for 0%

commit v1 on v0

--- a/solution.py
+++ b/solution.py
@@ -1,11 +1,16 @@
+import functools
 import math
 
 import jax
 import jax.numpy as jnp
 from jax import lax
+from jax.experimental import pallas as pl
+from jax.experimental.pallas import tpu as pltpu
 from jax.sharding import PartitionSpec as P
 
 HEAD_DIM = 128
+MESH = pl.DeviceIdType.MESH
+VMEM_BUDGET = 40 * 2**20
 
 
 def attend(queries, latent, key_basis, value_basis):
@@ -44,7 +49,7 @@
     return mixed.transpose(1, 0, 2).reshape(tok_rows, head_count * HEAD_DIM)
 
 
-def shards(queries, latent, key_basis, value_basis, out_weight):
+def collective_shards(queries, latent, key_basis, value_basis, out_weight):
     gathered = lax.all_gather(latent, "seq", axis=1, tiled=True)
     attended_heads = attend(queries, gathered, key_basis, value_basis)
     partial_value = lax.dot_general(
@@ -53,10 +58,278 @@
         (((1,), (1,)), ((), ())),
         preferred_element_type=jnp.float32,
     )
-    attended = lax.psum_scatter(partial_value, "head", scatter_dimension=1, tiled=True).astype(
+    return lax.psum_scatter(partial_value, "head", scatter_dimension=1, tiled=True).astype(
         jnp.bfloat16
     )
-    return attended
+
+
+def chunk_count(heads):
+    return next(c for c in (4, 3, 2, 1) if heads % c == 0)
+
+
+def kernel(
+    n,
+    q_hbm, lat_hbm, kb_hbm, vb_hbm, ow_hbm,
+    out_ref,
+    q_all, lat_all, kb, vb, ow, keys, values, part, swap, fin, landed,
+    local_sem, send_sem, recv_sem, swap_sem, fin_send, fin_recv,
+):
+    chunks, _, tok, width = q_all.shape
+    tokens = n * tok
+    rows = n // 2
+    heads = width // HEAD_DIM
+    score_scale = 1.0 / math.sqrt(HEAD_DIM)
+    me, core = lax.axis_index("seq"), lax.axis_index("head")
+    row, side = me // 2, me % 2
+    partner = row * 2 + (1 - side)
+
+    def column(j, which=side):
+        return ((row + j) % rows) * 2 + which
+
+    def to(seq, head=core):
+        return {"seq": seq, "head": head}
+
+    locals_ = [
+        pltpu.make_async_copy(lat_hbm, lat_all.at[me], local_sem.at[0]),
+        pltpu.make_async_copy(kb_hbm, kb, local_sem.at[1]),
+        pltpu.make_async_copy(vb_hbm, vb, local_sem.at[2]),
+        pltpu.make_async_copy(ow_hbm, ow, local_sem.at[3]),
+    ] + [
+        pltpu.make_async_copy(
+            q_hbm.at[:, pl.ds(c * width, width)], q_all.at[c, me], local_sem.at[4 + c]
+        )
+        for c in range(chunks)
+    ]
+    for copy in locals_:
+        copy.start()
+
+    barrier = pltpu.get_barrier_semaphore()
+    greet = [to(column(j)) for j in range(1, rows)] + [to(partner), to(me, 1 - core)]
+    for peer in greet:
+        pl.semaphore_signal(barrier, inc=1, device_id=peer, device_id_type=MESH)
+    pl.semaphore_wait(barrier, len(greet))
+
+    started = []
+
+    def piece(c, seq):
+        return lat_all.at[seq] if c == chunks else q_all.at[c, seq]
+
+    def send(c, src, seq, target, slot):
+        copy = pltpu.make_async_remote_copy(
+            src_ref=src,
+            dst_ref=piece(c, seq),
+            send_sem=send_sem.at[c, slot],
+            recv_sem=recv_sem.at[c, seq],
+            device_id=target,
+            device_id_type=MESH,
+        )
+        copy.start()
+        started.append(copy)
+
+    def arrived(c, seq):
+        pltpu.make_async_remote_copy(
+            src_ref=piece(c, seq),
+            dst_ref=piece(c, seq),
+            send_sem=send_sem.at[c, 0],
+            recv_sem=recv_sem.at[c, seq],
+            device_id=to(partner),
+            device_id_type=MESH,
+        ).wait_recv()
+
+    def spread(c, src):
+        for j in range(1, rows):
+            send(c, src, me, to(column(j)), j)
+        send(c, src, me, to(partner), 0)
+
+    def relay(c):
+        for j in range(1, rows):
+            arrived(c, column(j))
+            send(c, piece(c, column(j)), column(j), to(partner), rows - 1 + j)
+
+    spread(chunks, lat_hbm)
+    for c in range(chunks):
+        spread(c, q_hbm.at[:, pl.ds(c * width, width)])
+
+    relay(chunks)
+    for j in range(rows):
+        arrived(chunks, column(j, 1 - side))
+    locals_[0].wait()
+    latent = lat_all[...].reshape(tokens, lat_all.shape[2])
+    locals_[1].wait()
+    locals_[2].wait()
+    for c in range(chunks):
+        cols = pl.ds(c * width, width)
+        keys[c] = jnp.dot(latent, kb[:, cols], preferred_element_type=jnp.float32).astype(
+            jnp.bfloat16
+        )
+        values[c] = jnp.dot(latent, vb[:, cols], preferred_element_type=jnp.float32).astype(
+            jnp.bfloat16
+        )
+        relay(c)
+
+    locals_[3].wait()
+    total = None
+    for c in range(chunks):
+        for j in range(rows):
+            arrived(c, column(j, 1 - side))
+        locals_[4 + c].wait()
+        mixed = []
+        for h in range(heads):
+            cols = pl.ds(h * HEAD_DIM, HEAD_DIM)
+            query = q_all[c, :, :, cols].reshape(tokens, HEAD_DIM)
+            scores = (
+                lax.dot_general(
+                    query,
+                    keys[c, :, cols],
+                    (((1,), (1,)), ((), ())),
+                    preferred_element_type=jnp.float32,
+                )
+                * score_scale
+            )
+            weights = jnp.exp(scores - jnp.max(scores, axis=1, keepdims=True))
+            totals = jnp.sum(weights, axis=1, keepdims=True)
+            mixed.append(
+                (
+                    jnp.dot(
+                        weights.astype(jnp.bfloat16),
+                        values[c, :, cols],
+                        preferred_element_type=jnp.float32,
+                    )
+                    / totals
+                ).astype(jnp.bfloat16)
+            )
+        term = lax.dot_general(
+            jnp.concatenate(mixed, axis=1) if heads > 1 else mixed[0],
+            ow[:, pl.ds(c * width, width)],
+            (((1,), (1,)), ((), ())),
+            preferred_element_type=jnp.float32,
+        )
+        total = term if total is None else total + term
+
+    part[...] = total.reshape(part.shape)
+    exchange = pltpu.make_async_remote_copy(
+        src_ref=part.at[1 - core],
+        dst_ref=swap,
+        send_sem=swap_sem.at[0],
+        recv_sem=swap_sem.at[1],
+        device_id=to(me, 1 - core),
+        device_id_type=MESH,
+    )
+    exchange.start()
+    exchange.wait_recv()
+    fin[...] = (part[core] + swap[...]).astype(jnp.bfloat16).reshape(fin.shape)
+
+    slot, keeper = me % rows, me // rows
+    for j in range(rows):
+        owner = core * rows + j
+        here = jnp.logical_and(owner == me, keeper == core)
+        copy = pltpu.make_async_remote_copy(
+            src_ref=fin.at[j],
+            dst_ref=landed.at[slot],
+            send_sem=fin_send.at[j],
+            recv_sem=fin_recv.at[slot],
+            device_id=to(owner, keeper),
+            device_id_type=MESH,
+        )
+
+        @pl.when(jnp.logical_not(here))
+        def _():
+            copy.start()
+
+        @pl.when(here)
+        def _():
+            landed[slot] = fin[j]
+
+    own_here = me // rows == core
+    feats = landed.shape[2]
+    for i in range(rows):
+        @pl.when(jnp.logical_not(jnp.logical_and(own_here, i == slot)))
+        def _():
+            pltpu.make_async_remote_copy(
+                src_ref=landed.at[i],
+                dst_ref=landed.at[i],
+                send_sem=fin_send.at[0],
+                recv_sem=fin_recv.at[i],
+                device_id=to(partner),
+                device_id_type=MESH,
+            ).wait_recv()
+
+        out_ref[:, i * feats : (i + 1) * feats] = landed[i]
+
+    for copy in started:
+        copy.wait_send()
+    exchange.wait_send()
+    for j in range(rows):
+        owner = core * rows + j
+
+        @pl.when(jnp.logical_not(jnp.logical_and(owner == me, keeper == core)))
+        def _():
+            pltpu.make_async_remote_copy(
+                src_ref=fin.at[j],
+                dst_ref=landed.at[slot],
+                send_sem=fin_send.at[j],
+                recv_sem=fin_recv.at[slot],
+                device_id=to(owner, keeper),
+                device_id_type=MESH,
+            ).wait_send()
+
+
+def fused_shards(n, queries, latent, key_basis, value_basis, out_weight):
+    tok, local = queries.shape
+    rank = latent.shape[0]
+    feats = out_weight.shape[0]
+    chunks = chunk_count(local // HEAD_DIM)
+    width = local // chunks
+    rows = n // 2
+    tokens = n * tok
+    bf16, f32 = jnp.bfloat16, jnp.float32
+    hbm = pl.BlockSpec(memory_space=pl.ANY)
+    return pl.pallas_call(
+        functools.partial(kernel, n),
+        out_shape=jax.ShapeDtypeStruct((tok, rows * feats), bf16),
+        in_specs=[hbm] * 5,
+        out_specs=pl.BlockSpec(memory_space=pltpu.VMEM),
+        scratch_shapes=[
+            pltpu.VMEM((chunks, n, tok, width), bf16),
+            pltpu.VMEM((n, tok, rank), bf16),
+            pltpu.VMEM((rank, local), bf16),
+            pltpu.VMEM((rank, local), bf16),
+            pltpu.VMEM((feats, local), bf16),
+            pltpu.VMEM((chunks, tokens, width), bf16),
+            pltpu.VMEM((chunks, tokens, width), bf16),
+            pltpu.VMEM((2, tokens // 2, feats), f32),
+            pltpu.VMEM((tokens // 2, feats), f32),
+            pltpu.VMEM((rows, tok, feats), bf16),
+            pltpu.VMEM((rows, tok, feats), bf16),
+            pltpu.SemaphoreType.DMA((4 + chunks,)),
+            pltpu.SemaphoreType.DMA((chunks + 1, n)),
+            pltpu.SemaphoreType.DMA((chunks + 1, n)),
+            pltpu.SemaphoreType.DMA((2,)),
+            pltpu.SemaphoreType.DMA((rows,)),
+            pltpu.SemaphoreType.DMA((rows,)),
+        ],
+        compiler_params=pltpu.CompilerParams(collective_id=0, has_side_effects=True),
+        name="fused_attention",
+    )(queries, latent.T, key_basis, value_basis, out_weight)
+
+
+def shards(n, cores, queries, latent, key_basis, value_basis, out_weight):
+    tok, local = queries.shape
+    rank = latent.shape[0]
+    feats = out_weight.shape[0]
+    tokens = n * tok
+    held = 2 * (3 * tokens * local + tokens * rank + 2 * rank * local + feats * local)
+    held += 4 * (3 * tokens * feats + 3 * tokens * tokens)
+    if (
+        cores == 2
+        and n % 2 == 0
+        and tok % 16 == 0
+        and feats % 128 == 0
+        and rank % 128 == 0
+        and held <= VMEM_BUDGET
+    ):
+        return fused_shards(n, queries, latent, key_basis, value_basis, out_weight)
+    return collective_shards(queries, latent, key_basis, value_basis, out_weight)
 
 
 def solution(mesh):
@@ -68,5 +341,9 @@
         P("seq", "head"),
     )
     return jax.shard_map(
-        shards, mesh=mesh, in_specs=placed, out_specs=P(("groups", "seq"), "head"), check_vma=False
-    )
+        functools.partial(shards, mesh.shape["seq"], mesh.shape["head"]),
+        mesh=mesh,
+        in_specs=placed,
+        out_specs=P(("groups", "seq"), "head"),
+        check_vma=False,
+    )

time: 172 us -> 26.7 us (0.16)
  waiting for transfers between devices: 108 us -> 0 us
  blocking collectives: 26.8 us -> 0 us
  Pallas kernels: 0 us -> 25.2 us
  matrix products: 15.4 us -> 0 us
  between operations: 13.5 us -> 0.01 us
  other arithmetic: 3.78 us -> 0 us
  local copies, waits for them, and re-layouts: 3.65 us -> 1.42 us
    all_gather x1 -> x0, waiting for transfers between devices: 100 us -> none  [shards(): lax.all_gather(out_weight, 'seq', axis=0, tiled=True)]
    all_gather x1 -> x0, blocking collectives: 26.8 us -> none  [shards(): gathered = lax.all_gather(latent, 'seq', axis=1, tiled=True)]
    pallas_call x0 -> x1, Pallas kernels: none -> 25.2 us  [fused_shards(): pl.pallas_call(functools.partial(kernel, n), out_shape=jax.ShapeDtypeStru...]
    dot_general x25 -> x0, matrix products: 15.4 us -> none  [the longest x1 6.91 us: shards(): lax.dot_general(attended_heads, lax.all_gather(out_weight, 'seq', axis=0,...]
    reduce_scatter x1 -> x0, waiting for transfers between devices: 7.06 us -> none  [shards(): lax.psum_scatter(partial_value, 'head', scatter_dimension=1, tiled=True)]
    reduce_sum x12 -> x0, other arithmetic: 2.26 us -> none  [one_head(): row_total = jnp.sum(weights, axis=1, keepdims=True)]
    unnamed x6 -> x1, local copies, waits for them, and re-layouts: 3.46 us -> 1.42 us
  transfers between devices with their start and end apart: 2 -> 0, of which waited for: 2 -> 0; matrix products, arithmetic and copies ran while one was open for 8% -> 0% of each run, Pallas kernels for 0% -> 0%
where the time goes in v1:
time: 26.7 us; the launch traced here: 26.6 us
  Pallas kernels  25.2 us (94%)
  local copies, waits for them, and re-layouts  1.42 us (5%)
    pallas_call x1, Pallas kernels, fused_shards(): pl.pallas_call(functools.partial(kernel, n), out_shape=jax.ShapeDtypeStru...  25.2 us
    unnamed x1, local copies, waits for them, and re-layouts  1.42 us

profile of v1, /device:TPU:1, one launch (start us, length us, event | category | flops | bytes accessed | tf_op | source)
XLA Modules:
  0.0 26.6 jit_solution(9663880693806295237)
XLA Ops:
  0.0 25.2 %fused_attention.1 = bf16[16,1536]{1,0:T(8,128)(2,1)} custom-call(bf16[16,1536]{1,0:T(8,128)(2,1)} %q_hbm.1, bf16[16,512]{1,0:T(8,128)(2,1)} %bitcast.1, bf16[512,1536]{1,0:T(8,128)(2,1)} %kb_hbm.1, bf16[512,1536]{1,0:T(8,128)(2,1)} %vb_hbm.1, bf16[384,1536]{1,0:T(8,128)(2,1)} %ow_hbm.1), custom_call_target="tpu_custom_call" | custom-call | tf_op jit(solution)/shard_map/fused_attention/pallas_call | solution.py:287
  25.2 1.4 %copy.7 = bf16[16,1536]{1,0:T(8,128)(2,1)} copy(bf16[16,1536]{1,0:T(8,128)(2,1)} %fused_attention.1) | data formatting | bytes 98304

commit v2 on v1

--- a/solution.py
+++ b/solution.py
@@ -11,6 +11,7 @@
 HEAD_DIM = 128
 MESH = pl.DeviceIdType.MESH
 VMEM_BUDGET = 40 * 2**20
+DIRECT = 0
 
 
 def attend(queries, latent, key_basis, value_basis):
@@ -63,6 +64,16 @@
     )
 
 
+def other_row(row, rows, j):
+    reach = jnp.maximum(row, rows - 1 - row)
+    below = row * 2 > rows - 1
+    lone = jnp.abs(rows - 1 - 2 * row)
+    k = j - lone
+    distance = jnp.where(j < lone, reach - j, (reach - lone) - k // 2)
+    towards_low = jnp.where(j < lone, below, (k % 2 == 0) == below)
+    return jnp.where(towards_low, row - distance, row + distance)
+
+
 def chunk_count(heads):
     return next(c for c in (4, 3, 2, 1) if heads % c == 0)
 
@@ -71,7 +82,7 @@
     n,
     q_hbm, lat_hbm, kb_hbm, vb_hbm, ow_hbm,
     out_ref,
-    q_all, lat_all, kb, vb, ow, keys, values, part, swap, fin, landed,
+    q_all, lat_all, kb, vb, ow, keys, values, early, part, swap, fin, landed,
     local_sem, send_sem, recv_sem, swap_sem, fin_send, fin_recv,
 ):
     chunks, _, tok, width = q_all.shape
@@ -83,14 +94,13 @@
     row, side = me // 2, me % 2
     partner = row * 2 + (1 - side)
 
-    def column(j, which=side):
-        return ((row + j) % rows) * 2 + which
-
     def to(seq, head=core):
         return {"seq": seq, "head": head}
 
+    half = lat_all.shape[3]
+    mine = pl.ds(core * half, half)
     locals_ = [
-        pltpu.make_async_copy(lat_hbm, lat_all.at[me], local_sem.at[0]),
+        pltpu.make_async_copy(lat_hbm.at[:, mine], lat_all.at[core, me], local_sem.at[0]),
         pltpu.make_async_copy(kb_hbm, kb, local_sem.at[1]),
         pltpu.make_async_copy(vb_hbm, vb, local_sem.at[2]),
         pltpu.make_async_copy(ow_hbm, ow, local_sem.at[3]),
@@ -104,74 +114,99 @@
         copy.start()
 
     barrier = pltpu.get_barrier_semaphore()
-    greet = [to(column(j)) for j in range(1, rows)] + [to(partner), to(me, 1 - core)]
+    others = [other_row(row, rows, j) for j in range(rows - 1)]
+    greet = [to(r * 2 + x) for r in others for x in (side, 1 - side)]
+    greet += [to(partner), to(me, 1 - core)]
     for peer in greet:
         pl.semaphore_signal(barrier, inc=1, device_id=peer, device_id_type=MESH)
     pl.semaphore_wait(barrier, len(greet))
 
     started = []
 
-    def piece(c, seq):
-        return lat_all.at[seq] if c == chunks else q_all.at[c, seq]
-
-    def send(c, src, seq, target, slot):
+    def send(c, src, dst, seq, target, slot):
         copy = pltpu.make_async_remote_copy(
             src_ref=src,
-            dst_ref=piece(c, seq),
+            dst_ref=dst,
             send_sem=send_sem.at[c, slot],
             recv_sem=recv_sem.at[c, seq],
-            device_id=target,
+            device_id=to(target),
             device_id_type=MESH,
         )
         copy.start()
         started.append(copy)
 
     def arrived(c, seq):
+        block = lat_all.at[core, seq] if c == chunks else q_all.at[c, seq]
         pltpu.make_async_remote_copy(
-            src_ref=piece(c, seq),
-            dst_ref=piece(c, seq),
+            src_ref=block,
+            dst_ref=block,
             send_sem=send_sem.at[c, 0],
             recv_sem=recv_sem.at[c, seq],
             device_id=to(partner),
             device_id_type=MESH,
         ).wait_recv()
 
-    def spread(c, src):
-        for j in range(1, rows):
-            send(c, src, me, to(column(j)), j)
-        send(c, src, me, to(partner), 0)
+    peers = [r * 2 + x for r in others for x in (1 - side, side)] + [partner]
+    for i, peer in enumerate(peers):
+        send(chunks, lat_hbm.at[:, mine], lat_all.at[core, me], me, peer, i)
+    for c in range(chunks):
+        send(c, q_hbm.at[:, pl.ds(c * width, width)], q_all.at[c, me], me, partner, 0)
+    relayed = max(chunks - DIRECT, 0)
+    for c in range(chunks):
+        src = q_hbm.at[:, pl.ds(c * width, width)]
+        for j in range(rows - 1):
+            if c >= relayed:
+                send(c, src, q_all.at[c, me], me, others[j] * 2 + 1 - side, rows + j)
+            send(c, src, q_all.at[c, me], me, others[j] * 2 + side, 1 + j)
 
     def relay(c):
-        for j in range(1, rows):
-            arrived(c, column(j))
-            send(c, piece(c, column(j)), column(j), to(partner), rows - 1 + j)
-
-    spread(chunks, lat_hbm)
-    for c in range(chunks):
-        spread(c, q_hbm.at[:, pl.ds(c * width, width)])
-
-    relay(chunks)
-    for j in range(rows):
-        arrived(chunks, column(j, 1 - side))
+        for j in range(rows - 1):
+            seq = others[j] * 2 + side
+            arrived(c, seq)
+            if c < relayed:
+                send(c, q_all.at[c, seq], q_all.at[c, seq], seq, partner, rows + j)
+
+    for peer in peers:
+        arrived(chunks, peer)
     locals_[0].wait()
-    latent = lat_all[...].reshape(tokens, lat_all.shape[2])
+    share = pltpu.make_async_remote_copy(
+        src_ref=lat_all.at[core],
+        dst_ref=lat_all.at[core],
+        send_sem=swap_sem.at[2],
+        recv_sem=swap_sem.at[3],
+        device_id=to(me, 1 - core),
+        device_id_type=MESH,
+    )
+    share.start()
+
+    def decode(basis, which, c):
+        return jnp.dot(
+            lat_all[which].reshape(tokens, half),
+            basis[pl.ds(which * half, half), pl.ds(c * width, width)],
+            preferred_element_type=jnp.float32,
+        )
+
     locals_[1].wait()
     locals_[2].wait()
     for c in range(chunks):
-        cols = pl.ds(c * width, width)
-        keys[c] = jnp.dot(latent, kb[:, cols], preferred_element_type=jnp.float32).astype(
-            jnp.bfloat16
-        )
-        values[c] = jnp.dot(latent, vb[:, cols], preferred_element_type=jnp.float32).astype(
-            jnp.bfloat16
-        )
-        relay(c)
+        early[0, c] = decode(kb, core, c)
+        early[1, c] = decode(vb, core, c)
+        if c < relayed - 1:
+            relay(c)
+    share.wait_recv()
+    for c in range(chunks):
+        keys[c] = (early[0, c] + decode(kb, 1 - core, c)).astype(jnp.bfloat16)
+        values[c] = (early[1, c] + decode(vb, 1 - core, c)).astype(jnp.bfloat16)
+    if relayed:
+        relay(relayed - 1)
 
     locals_[3].wait()
     total = None
     for c in range(chunks):
-        for j in range(rows):
-            arrived(c, column(j, 1 - side))
+        if c >= relayed:
+            relay(c)
+        for r in range(rows):
+            arrived(c, r * 2 + 1 - side)
         locals_[4 + c].wait()
         mixed = []
         for h in range(heads):
@@ -220,7 +255,9 @@
     fin[...] = (part[core] + swap[...]).astype(jnp.bfloat16).reshape(fin.shape)
 
     slot, keeper = me % rows, me // rows
-    for j in range(rows):
+    flip = me < core * rows + rows // 2
+    for i in range(rows):
+        j = jnp.where(flip, rows - 1 - i, i)
         owner = core * rows + j
         here = jnp.logical_and(owner == me, keeper == core)
         copy = pltpu.make_async_remote_copy(
@@ -258,6 +295,7 @@
 
     for copy in started:
         copy.wait_send()
+    share.wait_send()
     exchange.wait_send()
     for j in range(rows):
         owner = core * rows + j
@@ -283,7 +321,7 @@
     rows = n // 2
     tokens = n * tok
     bf16, f32 = jnp.bfloat16, jnp.float32
-    hbm = pl.BlockSpec(memory_space=pl.ANY)
+    hbm = pl.BlockSpec(memory_space=pltpu.HBM)
     return pl.pallas_call(
         functools.partial(kernel, n),
         out_shape=jax.ShapeDtypeStruct((tok, rows * feats), bf16),
@@ -291,12 +329,13 @@
         out_specs=pl.BlockSpec(memory_space=pltpu.VMEM),
         scratch_shapes=[
             pltpu.VMEM((chunks, n, tok, width), bf16),
-            pltpu.VMEM((n, tok, rank), bf16),
+            pltpu.VMEM((2, n, tok, rank // 2), bf16),
             pltpu.VMEM((rank, local), bf16),
             pltpu.VMEM((rank, local), bf16),
             pltpu.VMEM((feats, local), bf16),
             pltpu.VMEM((chunks, tokens, width), bf16),
             pltpu.VMEM((chunks, tokens, width), bf16),
+            pltpu.VMEM((2, chunks, tokens, width), f32),
             pltpu.VMEM((2, tokens // 2, feats), f32),
             pltpu.VMEM((tokens // 2, feats), f32),
             pltpu.VMEM((rows, tok, feats), bf16),
@@ -304,13 +343,18 @@
             pltpu.SemaphoreType.DMA((4 + chunks,)),
             pltpu.SemaphoreType.DMA((chunks + 1, n)),
             pltpu.SemaphoreType.DMA((chunks + 1, n)),
-            pltpu.SemaphoreType.DMA((2,)),
+            pltpu.SemaphoreType.DMA((4,)),
             pltpu.SemaphoreType.DMA((rows,)),
             pltpu.SemaphoreType.DMA((rows,)),
         ],
-        compiler_params=pltpu.CompilerParams(collective_id=0, has_side_effects=True),
+        compiler_params=pltpu.CompilerParams(
+            collective_id=0, has_side_effects=True, vmem_limit_bytes=VMEM_BUDGET
+        ),
         name="fused_attention",
-    )(queries, latent.T, key_basis, value_basis, out_weight)
+    )(*(
+        pltpu.with_memory_space_constraint(x, pltpu.HBM)
+        for x in (queries, latent.T, key_basis, value_basis, out_weight)
+    ))
 
 
 def shards(n, cores, queries, latent, key_basis, value_basis, out_weight):
@@ -319,13 +363,13 @@
     feats = out_weight.shape[0]
     tokens = n * tok
     held = 2 * (3 * tokens * local + tokens * rank + 2 * rank * local + feats * local)
-    held += 4 * (3 * tokens * feats + 3 * tokens * tokens)
+    held += 4 * (2 * tokens * local + 3 * tokens * feats + 3 * tokens * tokens)
     if (
         cores == 2
         and n % 2 == 0
         and tok % 16 == 0
         and feats % 128 == 0
-        and rank % 128 == 0
+        and rank % 256 == 0
         and held <= VMEM_BUDGET
     ):
         return fused_shards(n, queries, latent, key_basis, value_basis, out_weight)

time: 26.7 us -> 22.8 us (0.85)
  Pallas kernels: 25.2 us -> 22 us
  local copies, waits for them, and re-layouts: 1.42 us -> 0.62 us
    pallas_call x1, Pallas kernels: 25.2 us -> 22 us  [fused_shards(): pl.pallas_call(functools.partial(kernel, n), out_shape=jax.ShapeDtypeStru...]
    unnamed x1, local copies, waits for them, and re-layouts: 1.42 us -> 0.62 us
where the time goes in v2:
time: 22.8 us; the launch traced here: 22.6 us
  Pallas kernels  22 us (96%)
  local copies, waits for them, and re-layouts  0.62 us (3%)
    pallas_call x1, Pallas kernels, fused_shards(): pl.pallas_call(functools.partial(kernel, n), out_shape=jax.ShapeDtypeStru...  22 us
    unnamed x1, local copies, waits for them, and re-layouts  0.62 us

profile of v2, /device:TPU:1, one launch (start us, length us, event | category | flops | bytes accessed | tf_op | source)
XLA Modules:
  0.0 22.6 jit_solution(8578143487265648145)
XLA Ops:
  0.0 22.0 %fused_attention.1 = bf16[16,1536]{1,0:T(8,128)(2,1)S(1)} custom-call(bf16[16,1536]{1,0:T(8,128)(2,1)} %q_hbm.1, bf16[16,512]{1,0:T(8,128)(2,1)} %bitcast.1, bf16[512,1536]{1,0:T(8,128)(2,1)} %kb_hbm.1, bf16[512,1536]{1,0:T(8,128)(2,1)} %vb_hbm.1, bf16[384,1536]{1,0:T(8,128)(2,1)} %ow_hbm.1), custom_call_target="tpu_custom_call" | custom-call | tf_op jit(solution)/shard_map/fused_attention/pallas_call | solution.py:325
  22.0 0.6 %copy.7 = bf16[16,1536]{1,0:T(8,128)(2,1)} copy(bf16[16,1536]{1,0:T(8,128)(2,1)S(1)} %fused_attention.1) | data formatting | bytes 98304

commit v3 on v2

--- a/solution.py
+++ b/solution.py
@@ -110,15 +110,14 @@
         )
         for c in range(chunks)
     ]
-    for copy in locals_:
-        copy.start()
-
     barrier = pltpu.get_barrier_semaphore()
     others = [other_row(row, rows, j) for j in range(rows - 1)]
     greet = [to(r * 2 + x) for r in others for x in (side, 1 - side)]
     greet += [to(partner), to(me, 1 - core)]
     for peer in greet:
         pl.semaphore_signal(barrier, inc=1, device_id=peer, device_id_type=MESH)
+    for copy in locals_:
+        copy.start()
     pl.semaphore_wait(barrier, len(greet))
 
     started = []
@@ -160,7 +159,7 @@
             send(c, src, q_all.at[c, me], me, others[j] * 2 + side, 1 + j)
 
     def relay(c):
-        for j in range(rows - 1):
+        for j in reversed(range(rows - 1)):
             seq = others[j] * 2 + side
             arrived(c, seq)
             if c < relayed:

time: 22.8 us -> 22.8 us (level)
  no operation moved by 1% of the time
where the time goes in v3:
time: 22.8 us; the launch traced here: 22.6 us
  Pallas kernels  22 us (96%)
  local copies, waits for them, and re-layouts  0.62 us (3%)
    pallas_call x1, Pallas kernels, fused_shards(): pl.pallas_call(functools.partial(kernel, n), out_shape=jax.ShapeDtypeStru...  22 us
    unnamed x1, local copies, waits for them, and re-layouts  0.62 us

profile of v3, /device:TPU:1, one launch (start us, length us, event | category | flops | bytes accessed | tf_op | source)
XLA Modules:
  0.0 22.6 jit_solution(18324098332330375350)
XLA Ops:
  0.0 22.0 %fused_attention.1 = bf16[16,1536]{1,0:T(8,128)(2,1)S(1)} custom-call(bf16[16,1536]{1,0:T(8,128)(2,1)} %q_hbm.1, bf16[16,512]{1,0:T(8,128)(2,1)} %bitcast.1, bf16[512,1536]{1,0:T(8,128)(2,1)} %kb_hbm.1, bf16[512,1536]{1,0:T(8,128)(2,1)} %vb_hbm.1, bf16[384,1536]{1,0:T(8,128)(2,1)} %ow_hbm.1), custom_call_target="tpu_custom_call" | custom-call | tf_op jit(solution)/shard_map/fused_attention/pallas_call | solution.py:324
  22.0 0.6 %copy.7 = bf16[16,1536]{1,0:T(8,128)(2,1)} copy(bf16[16,1536]{1,0:T(8,128)(2,1)S(1)} %fused_attention.1) | data formatting | bytes 98304
